TPU v7x, 512 devices: a whole 4x8x8 slice. The times are simulated.
512 devices in a mesh: wide: 64 (over y, x, core), freq: 8 (over z).
Axes of the slice: x: 4, y: 8, z: 8, core: 2. Of those that a mesh axis runs over, the one named last changes fastest.
Arguments:
- wave: bfloat16 [2, 8, 1024, 1024], P(None, 'freq', 'wide'), may hold values from -6 to 6
- filters: bfloat16 [2, 2, 8, 3, 81], P(None, None, 'freq'), may hold values from -0.6640625 to 0.6640625
- vel_bins: int32 [2, 2, 3, 1024], replicated, may hold values from 0 to 2
- blend_levels: int32 [2, 2, 3, 1024], replicated, may hold values from 1 to 16
- aperture: int32 [2, 64, 64], replicated, may hold values 0 or 1
Outputs:
- image_shallow: float32 [1024, 1024], P('wide', 'freq')
- image_deep: float32 [1024, 1024], P('wide', 'freq')
All inputs are finite; a program needn't handle non-finite values.
Results may differ from a plain program's by a relative error of at most 0.017.
Values may be sent and summed in bfloat16 or wider, within the bound.
A program may use at most 64 MiB of HBM per device.

v0:
```python
import jax
import jax.numpy as jnp
from jax import lax
from jax.sharding import PartitionSpec as P

SIDE = 32
TAPS = 9
VBINS = 3
BLK = 16


def in_blocks(shard, dim, devices):
    before, after = (shard.shape[:dim], shard.shape[dim + 1 :])
    return jnp.moveaxis(shard.reshape(*before, devices, -1, *after), dim, 0)


def summed_on_arrival(shard, axis, dim):
    blocks = in_blocks(shard, dim, lax.axis_size(axis))
    arrived = lax.all_to_all(blocks, axis, split_axis=0, concat_axis=0, tiled=True)
    return arrived.astype(jnp.float32).sum(axis=0)


def blend_table(bin_ids, levels):
    weights = levels.astype(jnp.float32)
    onehot = (bin_ids[:, None, :] == jnp.arange(VBINS, dtype=jnp.int32)[None, :, None]).astype(
        jnp.float32
    )
    return jnp.sum(onehot * weights[:, None, :], axis=0) / jnp.sum(weights, axis=0)[None, :]


def banded_bins(field_item, filt_real, filt_imag, table):
    rows_tile = max(1, 128 // SIDE)
    window = rows_tile + TAPS - 1
    tile_count = SIDE // rows_tile
    half_taps = TAPS // 2
    tap_range = jnp.arange(TAPS)[None, None, :]
    row_pick = (
        jnp.arange(window)[:, None, None] - jnp.arange(rows_tile)[None, :, None] == tap_range
    ).astype(jnp.float32)
    col_pick = (
        jnp.arange(SIDE)[:, None, None] - jnp.arange(SIDE)[None, :, None] + half_taps == tap_range
    ).astype(jnp.float32)

    def spread(filt_part):
        taps_grid = filt_part.reshape(VBINS, TAPS, TAPS).astype(jnp.float32)
        banded = jnp.einsum("iya,jxb,kab->kijyx", row_pick, col_pick, taps_grid)
        return banded.reshape(VBINS, window * SIDE, rows_tile * SIDE)

    band_real = spread(filt_real)
    band_imag = spread(filt_imag)
    upper_half = jnp.stack([band_real, band_imag], 1)
    lower_half = jnp.stack([-band_imag, band_real], 1)
    matrix = jnp.stack([upper_half, lower_half], 0)
    matrix = (
        jnp.transpose(matrix, (0, 3, 1, 2, 4))
        .reshape(2 * window * SIDE, VBINS * 2 * rows_tile * SIDE)
        .astype(jnp.bfloat16)
    )
    batch_rows = field_item.shape[1]
    grid_field = field_item.reshape(2, batch_rows, SIDE, SIDE)
    padded = jnp.pad(grid_field, ((0, 0), (0, 0), (half_taps, half_taps), (0, 0)))
    pieces = jnp.stack(
        [
            padded[:, :, tile_index * rows_tile : tile_index * rows_tile + window, :]
            for tile_index in range(tile_count)
        ],
        2,
    )
    pieces = jnp.transpose(pieces, (1, 2, 0, 3, 4)).reshape(
        batch_rows, tile_count, 2 * window * SIDE
    )
    product = jnp.dot(pieces, matrix, preferred_element_type=jnp.float32)
    product = product.reshape(batch_rows, tile_count, VBINS, 2, rows_tile * SIDE)
    weights = table.reshape(VBINS, tile_count, rows_tile * SIDE)
    return jnp.einsum("bnkct,knt->cbnt", product, weights).reshape(2, batch_rows, SIDE * SIDE)


def extrapolate(field, filters_now, table):
    blended = banded_bins(field[:, 0], filters_now[0, 0], filters_now[1, 0], table)
    members = [blended.astype(jnp.bfloat16)]
    return jnp.stack(members, 1)


def local_aperture(blocks, offset, row_count):
    picked = lax.dynamic_slice_in_dim(blocks, offset // BLK, row_count // BLK, 0)
    return jnp.repeat(jnp.repeat(picked, BLK, axis=0), BLK, axis=1)


def body(wave, filters, vel_bins, blend_levels, aperture):
    source_rows = wave.shape[2]
    offset = lax.axis_index("wide") * source_rows
    first = extrapolate(wave, filters[0], blend_table(vel_bins[0, 0], blend_levels[0, 0]))
    moved = lax.all_to_all(first, "wide", split_axis=3, concat_axis=2, tiled=True)
    second = extrapolate(
        jnp.swapaxes(moved, 2, 3), filters[0], blend_table(vel_bins[0, 1], blend_levels[0, 1])
    )
    keep_mask = local_aperture(aperture[0].T, offset, source_rows)
    shallow_field = jnp.where(keep_mask[None, None] > 0, second, jnp.zeros_like(second))
    shallow_part = jnp.sum(shallow_field[0].astype(jnp.float32), axis=0)
    image_shallow = summed_on_arrival(shallow_part.astype(jnp.bfloat16), "freq", 1)
    third = extrapolate(shallow_field, filters[1], blend_table(vel_bins[1, 1], blend_levels[1, 1]))
    returned = lax.all_to_all(third, "wide", split_axis=3, concat_axis=2, tiled=True)
    fourth = extrapolate(
        jnp.swapaxes(returned, 2, 3), filters[1], blend_table(vel_bins[1, 0], blend_levels[1, 0])
    )
    keep_mask = local_aperture(aperture[1], offset, source_rows)
    deep_field = jnp.where(keep_mask[None, None] > 0, fourth, jnp.zeros_like(fourth))
    deep_part = jnp.sum(deep_field[0].astype(jnp.float32), axis=0)
    image_deep = summed_on_arrival(deep_part.astype(jnp.bfloat16), "freq", 1)
    return (image_shallow, image_deep)


def solution(mesh):
    return jax.shard_map(
        body,
        mesh=mesh,
        in_specs=(P(None, "freq", "wide", None), P(None, None, "freq", None, None), P(), P(), P()),
        out_specs=(P("wide", "freq"), P("wide", "freq")),
        check_vma=False,
    )
```

profile of v0, /device:TPU:1, one launch (start us, length us, event | category | flops | bytes accessed | tf_op | source)
XLA Modules:
  0.0 117.5 jit_solution(6869207140005902294)
XLA Ops:
  0.7 1.5 %slice_convert_fusion = (f32[1,1,3,1024]{3,1,2,0:T(1,128)}, f32[1,1,3,1024]{3,1,2,0:T(1,128)S(1)}, f32[1,1,3,1024]{3,1,2,0:T(1,128)S(1)}, f32[1,1,3,1024]{3,1,2,0:T(1,128)}) fusion(s32[2,2,3,1024]{3,1,2,0:T(2,128)} %param.8), kind=kLoop, calls=%fused_computation.166 | loop fusion | flops 12288 | bytes 98304 | tf_op jit(solution)/shard_map/convert_element_type | solution.py:24
  2.1 1.5 %fusion.104 = (f32[1024]{0:T(1024)}, f32[1024]{0:T(1024)}, f32[1024]{0:T(1024)S(1)}, f32[1024]{0:T(1024)}) fusion(s32[2,2,3,1024]{3,1,2,0:T(2,128)} %param.8), kind=kLoop, calls=%fused_computation.179 | loop fusion | flops 20480 | bytes 65536 | tf_op jit(solution)/shard_map/reduce_sum | solution.py:28
  3.6 0.8 slice_reduce_fusion
  4.5 0.7 convert_bitcast_fusion.1
  5.2 1.9 %copy.137 = bf16[3,12,32,4,32]{4,3,2,1,0:T(4,128)(2,1)} copy(bf16[3,12,32,4,32]{4,1,2,3,0:T(8,128)(2,1)S(1)} %get-tuple-element.12) | data formatting | bytes 589824 | tf_op jit(solution)/shard_map/convert.15
  7.2 2.0 %reshape.272 = bf16[3,1,384,128]{3,2,0,1:T(8,128)(2,1)S(1)} reshape(bf16[3,12,32,4,32]{4,3,2,1,0:T(4,128)(2,1)} %copy.137) | data formatting | bytes 589824 | tf_op jit(solution)/shard_map/convert.15
  9.2 0.9 copy.138
  10.1 0.6 reshape.277
  10.8 0.7 fusion.2
  11.5 0.9 copy.136
  12.4 0.6 reshape.271
  13.3 1.2 %copy.139 = bf16[2,384,3,2,128]{4,3,2,1,0:T(2,128)(2,1)S(1)} copy(bf16[2,384,3,2,128]{4,1,2,3,0:T(8,128)(2,1)S(1)} %maximum_bitcast_fusion) | data formatting | bytes 2359296 | tf_op jit(solution)/shard_map/convert_element_type | solution.py:57
  14.5 0.6 convert_element_type.175
  15.1 0.6 copy.140
  16.5 0.8 reshape.285
  17.3 0.6 fusion.106
  18.0 0.6 copy_bitcast_fusion.7
  18.6 0.5 fusion.8
  19.2 0.3 copy.245
  19.5 1.1 reshape.317
  20.6 11.8 %all-to-all-start = ((bf16[64,2,256]{2,1,0:T(2,128)(2,1)}), bf16[64,2,256]{2,1,0:T(2,128)(2,1)}, u32[]{:S(2)}, u32[]{:S(2)}) async-start(bf16[64,2,256]{2,1,0:T(2,128)(2,1)} %reshape.317), calls=%async_computation | async-start | bytes 131072 | tf_op jit(solution)/shard_map/all_to_all | solution.py:93
  32.4 0.6 fusion.105
  33.4 0.7 copy.153
  34.2 1.9 %convert_bitcast_fusion = (bf16[3,12,32,4,32]{4,1,2,3,0:T(8,128)(2,1)}, bf16[3,12,32,4,32]{4,1,2,3,0:T(8,128)(2,1)S(1)}) fusion(s32[32,32]{1,0:T(8,128)S(1)} %subtract_add_fusion, s32[12,4]{0,1:T(4,128)S(1)} %iota_subtract_fusion, bf16[3,9,9,1]{2,1,0,3:T(8,128)(2,1)S(1)} %reshape.294), kind=kOutput, calls=%fused_computation.6 | convolution fusion | flops 3129552 | bytes 594598 | tf_op jit(solution)/shard_map/iya,jxb,kab->kijyx/dot_general | solution.py:46
  36.1 3.3 %copy.163 = bf16[3,12,32,4,32]{4,3,2,1,0:T(4,128)(2,1)} copy(bf16[3,12,32,4,32]{4,1,2,3,0:T(8,128)(2,1)} %get-tuple-element.10) | data formatting | bytes 589824 | tf_op jit(solution)/shard_map/convert.7
  39.4 2.0 %reshape.275 = bf16[3,1,384,128]{3,2,0,1:T(8,128)(2,1)S(1)} reshape(bf16[3,12,32,4,32]{4,3,2,1,0:T(4,128)(2,1)} %copy.163) | data formatting | bytes 589824 | tf_op jit(solution)/shard_map/convert.7
  41.5 1.9 %copy.164 = bf16[3,12,32,4,32]{4,3,2,1,0:T(4,128)(2,1)} copy(bf16[3,12,32,4,32]{4,1,2,3,0:T(8,128)(2,1)S(1)} %get-tuple-element.11) | data formatting | bytes 589824 | tf_op jit(solution)/shard_map/convert.3
  43.4 2.0 %reshape.278 = bf16[3,1,384,128]{3,2,0,1:T(8,128)(2,1)S(1)} reshape(bf16[3,12,32,4,32]{4,3,2,1,0:T(4,128)(2,1)} %copy.164) | data formatting | bytes 589824 | tf_op jit(solution)/shard_map/convert.3
  45.5 0.7 fusion.3
  46.3 1.9 %copy.162 = bf16[3,12,32,4,32]{4,3,2,1,0:T(4,128)(2,1)} copy(bf16[3,12,32,4,32]{4,1,2,3,0:T(8,128)(2,1)S(1)} %fusion.3) | data formatting | bytes 589824 | tf_op jit(solution)/shard_map/convert.6
  48.2 2.0 %reshape.274 = bf16[3,1,384,128]{3,2,0,1:T(8,128)(2,1)S(1)} reshape(bf16[3,12,32,4,32]{4,3,2,1,0:T(4,128)(2,1)} %copy.162) | data formatting | bytes 589824 | tf_op jit(solution)/shard_map/convert.6
  50.5 1.2 %copy.165 = bf16[2,384,3,2,128]{4,3,2,1,0:T(2,128)(2,1)S(1)} copy(bf16[2,384,3,2,128]{4,1,2,3,0:T(8,128)(2,1)S(1)} %maximum_bitcast_fusion.1) | data formatting | bytes 2359296 | tf_op jit(solution)/shard_map/convert_element_type | solution.py:57
  51.7 0.6 convert_element_type.189
  52.3 0.6 copy.166
  52.9 0.7 compare_bitcast_fusion
  53.8 0.7 broadcast_in_dim.18
  54.6 0.8 select_reduce_fusion.3
  55.3 0.7 fusion.92
  56.0 0.7 copy_bitcast_fusion.2
  56.8 0.7 copy_bitcast_fusion.3
  57.5 0.7 fusion.89
  58.2 0.7 fusion.90
  58.9 1.2 %reshape.318 = bf16[1024,1,2,16]{3,2,1,0:T(2,128)(2,1)S(1)} reshape(bf16[64,2,256]{2,1,0:T(2,128)(2,1)} %all-to-all-done) | data formatting | bytes 131072
  60.4 0.8 all_to_all.35
  61.7 1.0 copy-done
  62.7 2.4 %reshape.289 = bf16[16,8,768,1,1]{2,1,0,3,4:T(8,128)(2,1)S(1)} reshape(bf16[16,8,2,12,32]{4,3,2,1,0:T(8,128)(2,1)} %bitcast.438) | data formatting | bytes 393216 | tf_op jit(solution)/shard_map/reshape | solution.py:69
  65.0 0.5 fusion.9
  66.2 0.8 reshape.296
  67.0 0.5 fusion.10
  67.9 1.1 reshape.319
  69.0 10.3 %all-to-all-start.2 = ((bf16[64,2,256]{2,1,0:T(2,128)(2,1)}), bf16[64,2,256]{2,1,0:T(2,128)(2,1)S(1)}, u32[]{:S(2)}, u32[]{:S(2)}) async-start(bf16[64,2,256]{2,1,0:T(2,128)(2,1)} %reshape.319), calls=%async_computation.2 | async-start | bytes 131072 | tf_op jit(solution)/shard_map/all_to_all | solution.py:102
  79.3 0.6 copy.151
  79.9 9.4 %all-to-all-done.2 = bf16[64,2,256]{2,1,0:T(2,128)(2,1)S(1)} async-done(((bf16[64,2,256]{2,1,0:T(2,128)(2,1)}), bf16[64,2,256]{2,1,0:T(2,128)(2,1)S(1)}, u32[]{:S(2)}, u32[]{:S(2)}) %all-to-all-start.2) | async-done | bytes 65568 | tf_op jit(solution)/shard_map/all_to_all | solution.py:102
  89.4 10.0 %all-to-all-start.1 = ((bf16[8,16,128]{2,1,0:T(8,128)(2,1)}), bf16[8,16,128]{2,1,0:T(8,128)(2,1)S(1)}, u32[]{:S(2)}, u32[]{:S(2)}) async-start(bf16[8,16,128]{2,1,0:T(8,128)(2,1)} %copy.151), calls=%async_computation.1 | async-start | bytes 65536 | tf_op jit(solution)/shard_map/all_to_all | solution.py:19
  99.4 0.4 reshape.320
  100.0 0.8 all_to_all.40
  101.3 0.8 reshape.300
  102.1 0.5 fusion.11
  102.7 0.6 copy.177
  103.3 3.0 %all-to-all-done.1 = bf16[8,16,128]{2,1,0:T(8,128)(2,1)S(1)} async-done(((bf16[8,16,128]{2,1,0:T(8,128)(2,1)}), bf16[8,16,128]{2,1,0:T(8,128)(2,1)S(1)}, u32[]{:S(2)}, u32[]{:S(2)}) %all-to-all-start.1) | async-done | bytes 32800 | tf_op jit(solution)/shard_map/all_to_all | solution.py:19
  106.4 3.6 %all-to-all-start.3 = ((bf16[8,16,128]{2,1,0:T(8,128)(2,1)}), bf16[8,16,128]{2,1,0:T(8,128)(2,1)S(1)}, u32[]{:S(2)}, u32[]{:S(2)}) async-start(bf16[8,16,128]{2,1,0:T(8,128)(2,1)} %copy.177), calls=%async_computation.3 | async-start | bytes 65536 | tf_op jit(solution)/shard_map/all_to_all | solution.py:19
  110.0 0.6 convert_reduce_fusion.1
  110.6 6.3 %all-to-all-done.3 = bf16[8,16,128]{2,1,0:T(8,128)(2,1)S(1)} async-done(((bf16[8,16,128]{2,1,0:T(8,128)(2,1)}), bf16[8,16,128]{2,1,0:T(8,128)(2,1)S(1)}, u32[]{:S(2)}, u32[]{:S(2)}) %all-to-all-start.3) | async-done | bytes 32800 | tf_op jit(solution)/shard_map/all_to_all | solution.py:19
  116.9 0.6 convert_reduce_fusion
  (83 shorter events, 4.5 us)
Async XLA Ops:
  15.1 0.8 copy-start.1
  16.3 1.0 copy-start.3
  18.6 13.8 %copy-start.2 = (s32[2,64,64]{2,1,0:T(8,128)S(1)}, s32[2,64,64]{2,1,0:T(8,128)}, u32[]{:S(2)}) copy-start(s32[2,64,64]{2,1,0:T(8,128)} %param.9) | copy-start | bytes 98308
  20.6 38.4 %all-to-all-start = ((bf16[64,2,256]{2,1,0:T(2,128)(2,1)}), bf16[64,2,256]{2,1,0:T(2,128)(2,1)}, u32[]{:S(2)}, u32[]{:S(2)}) async-start(bf16[64,2,256]{2,1,0:T(2,128)(2,1)} %reshape.317), calls=%async_computation | async-start | bytes 131072 | tf_op jit(solution)/shard_map/all_to_all | solution.py:93
  33.2 0.9 copy-start.5
  61.7 1.0 copy-start
  65.0 0.8 copy-start.4
  69.0 20.4 %all-to-all-start.2 = ((bf16[64,2,256]{2,1,0:T(2,128)(2,1)}), bf16[64,2,256]{2,1,0:T(2,128)(2,1)S(1)}, u32[]{:S(2)}, u32[]{:S(2)}) async-start(bf16[64,2,256]{2,1,0:T(2,128)(2,1)} %reshape.319), calls=%async_computation.2 | async-start | bytes 131072 | tf_op jit(solution)/shard_map/all_to_all | solution.py:102
  89.4 17.0 %all-to-all-start.1 = ((bf16[8,16,128]{2,1,0:T(8,128)(2,1)}), bf16[8,16,128]{2,1,0:T(8,128)(2,1)S(1)}, u32[]{:S(2)}, u32[]{:S(2)}) async-start(bf16[8,16,128]{2,1,0:T(8,128)(2,1)} %copy.151), calls=%async_computation.1 | async-start | bytes 65536 | tf_op jit(solution)/shard_map/all_to_all | solution.py:19
  106.4 10.5 %all-to-all-start.3 = ((bf16[8,16,128]{2,1,0:T(8,128)(2,1)}), bf16[8,16,128]{2,1,0:T(8,128)(2,1)S(1)}, u32[]{:S(2)}, u32[]{:S(2)}) async-start(bf16[8,16,128]{2,1,0:T(8,128)(2,1)} %copy.177), calls=%async_computation.3 | async-start | bytes 65536 | tf_op jit(solution)/shard_map/all_to_all | solution.py:19
where the time goes:
time: 119 us; the launch traced here: 117 us
  local copies, waits for them, and re-layouts  47 us (39%)
  starting transfers between devices  35.8 us (30%)
  waiting for transfers between devices  18.7 us (16%)
  other arithmetic  8.41 us (7%)
  matrix products  6.25 us (5%)
  between operations  1.28 us (1%)
    another operation x12, local copies, waits for them, and re-layouts  20.2 us
    all_to_all x2, starting transfers between devices, summed_on_arrival(): lax.all_to_all(blocks, axis, split_axis=0, concat_axis=0, tiled=True)  13.7 us
    all_to_all x1, starting transfers between devices, body(): lax.all_to_all(first, 'wide', split_axis=3, concat_axis=2, tiled=True)  11.8 us
    all_to_all x1, starting transfers between devices, body(): lax.all_to_all(third, 'wide', split_axis=3, concat_axis=2, tiled=True)  10.3 us
    all_to_all x1, waiting for transfers between devices, body(): lax.all_to_all(third, 'wide', split_axis=3, concat_axis=2, tiled=True)  9.45 us
    all_to_all x2, waiting for transfers between devices, summed_on_arrival(): lax.all_to_all(blocks, axis, split_axis=0, concat_axis=0, tiled=True)  9.29 us
    unnamed x52, local copies, waits for them, and re-layouts  8.76 us
    reshape x4, local copies, waits for them, and re-layouts, banded_bins(): jnp.transpose(pieces, (1, 2, 0, 3, 4))  4.82 us
  transfers between devices with their start and end apart: 4, of which 3 were waited for; matrix products, arithmetic and copies ran while one was open for 26% of the time, Pallas kernels for 0%

commit v1 on v0

v1 whole, which is shorter than its diff:
```python
import functools

import jax
import jax.numpy as jnp
from jax import lax
from jax.experimental import pallas as pl
from jax.experimental.pallas import tpu as pltpu
from jax.sharding import PartitionSpec as P

SIDE = 32
TAPS = 9
VBINS = 3
BLK = 16
LANES = 128
WIN = 3 * LANES
HALF = TAPS // 2
MESH = pl.DeviceIdType.MESH
F32 = jnp.float32
BF16 = jnp.bfloat16


def iota(shape, dim):
    return lax.broadcasted_iota(jnp.int32, shape, dim)


def one_hot(rows, cols, target):
    return jnp.where(iota((rows, cols), 0) == target, 1.0, 0.0).astype(BF16)


def kernel(
    nt, wave_h, filt_h, bins_h, lev_h, ap_h, shal_o, deep_o,
    wave_v, filt_v, bins_v, lev_v, ap_v, taps_v, band_n, band_t, tab_r, tab_c, mask_s, mask_d,
    send1, ubuf, vbuf, send4, rbuf, dsend, drecv, ssend, srecv,
    in_sem, s1, r1, hs, hr, gs, gr, s4, r4, s5, r5, s6, r6, hub_sem,
):
    sb = LANES // nt
    w = lax.axis_index("wide")
    z = lax.axis_index("freq")
    y = w // nt
    xc = w % nt
    last = nt - 1

    def dev(yy, cc, zz):
        return (yy * nt + cc, zz)

    def remote(src, dst, ssem, rsem, to):
        return pltpu.make_async_remote_copy(
            src_ref=src, dst_ref=dst, send_sem=ssem, recv_sem=rsem, device_id=to, device_id_type=MESH
        )

    barrier = pltpu.get_barrier_semaphore()
    for k in range(1, nt):
        for to in (dev(y, (xc + k) % nt, z), dev((y + k) % nt, xc, z), dev(y, xc, (z + k) % nt)):
            pl.semaphore_signal(barrier, inc=1, device_id=to, device_id_type=MESH)

    loads = [
        pltpu.make_async_copy(h, v, in_sem.at[i])
        for i, (h, v) in enumerate(
            ((filt_h, filt_v), (wave_h, wave_v), (bins_h, bins_v), (lev_h, lev_v), (ap_h, ap_v))
        )
    ]
    for load in loads:
        load.start()

    taps_v[...] = jnp.zeros_like(taps_v)
    near = jnp.abs(iota((SIDE, LANES), 1) % SIDE - iota((SIDE, LANES), 0)) <= HALF
    loads[0].wait()
    for t in range(2):
        for k in range(VBINS):
            taps_v[pl.ds(2 * (VBINS * t + k), 2), pl.ds(0, TAPS * TAPS)] = filt_v[t, k].astype(F32)
    taps = taps_v[...].astype(BF16)

    def spread(rows, col_shift, flip):
        cols = iota((1, 12 * LANES), 1)
        group, m = cols // LANES, (cols + HALF) % LANES
        step, off = m // SIDE, m % SIDE
        a, b = (group - step, 2 * HALF - off) if flip else (4 * (group % 3) + step - group // 3, off)
        good = (a >= 0) & (a < TAPS) & (b >= 0) & (b < TAPS)
        target = jnp.where(good, a * TAPS + b, -1)
        return jnp.dot(taps, one_hot(LANES, 12 * LANES, target), preferred_element_type=F32)

    def banded(row):
        wide = jnp.broadcast_to(row, (SIDE, LANES))
        rolled = pltpu.roll(wide, 0, 1, stride=1, stride_axis=0)
        return jnp.where(near, rolled, 0.0).astype(BF16)

    def build_n(t, rows):
        for part in range(2):
            for k in range(VBINS):
                r = 2 * (VBINS * t + k) + part
                for i in range(12):
                    band_n[t, k, pl.ds(SIDE * i, SIDE), pl.ds(LANES * part, LANES)] = banded(
                        rows[r : r + 1, LANES * i : LANES * (i + 1)]
                    )

    def build_t(t, rows):
        for part in range(2):
            for k in range(VBINS):
                r = 2 * (VBINS * t + k) + part
                for j in range(4):
                    for q in range(3):
                        g = 3 * j + q
                        band_t[t, k, pl.ds(LANES * part + SIDE * j, SIDE), pl.ds(LANES * q, LANES)] = banded(
                            rows[r : r + 1, LANES * g : LANES * (g + 1)]
                        )

    def table(t, q, cols):
        bin_ids = [bins_v[t, j, pl.ds(q, 1), cols] for j in range(VBINS)]
        levels = [lev_v[t, j, pl.ds(q, 1), cols].astype(F32) for j in range(VBINS)]
        total = levels[0] + levels[1] + levels[2]
        rows = []
        for k in range(VBINS):
            hits = [jnp.where(b == k, v, 0.0) for b, v in zip(bin_ids, levels)]
            rows.append((hits[0] + hits[1] + hits[2]) / total)
        return rows

    def table_rows(t):
        for k, row in enumerate(table(t, 0, slice(None))):
            tab_r[t, pl.ds(k, 1), :] = row

    def table_cols(t):
        here = pl.ds(pl.multiple_of(y * LANES, LANES), LANES)
        for k, row in enumerate(table(t, 1, here)):
            tab_c[t, k] = jnp.transpose(jnp.broadcast_to(row, (LANES, LANES)))

    def over_r(field, t, parts):
        zero = jnp.zeros((sb, LANES), BF16)
        rows = []
        for c in range(2):
            for n in range(nt):
                rows.append(
                    jnp.concatenate(
                        [field(c, m) if 0 <= m < nt else zero for m in (n - 1, n, n + 1)], axis=1
                    )
                )
        lhs = jnp.concatenate(rows, axis=0)
        out = [[None] * nt for _ in range(parts)]
        for k in range(VBINS):
            prod = jnp.dot(lhs, band_n[t, k], preferred_element_type=F32)
            for n in range(nt):
                weight = tab_r[t, pl.ds(k, 1), pl.ds(LANES * n, LANES)]
                top = slice(sb * n, sb * (n + 1))
                low = slice(sb * (nt + n), sb * (nt + n + 1))
                terms = [prod[top, :LANES] - prod[low, LANES:]]
                if parts == 2:
                    terms.append(prod[top, LANES:] + prod[low, :LANES])
                for c, term in enumerate(terms):
                    term = weight * term
                    out[c][n] = term if k == 0 else out[c][n] + term
        return out

    def over_s(buf, t):
        rhs = jnp.concatenate(
            [
                jnp.concatenate([buf[q, :, c].reshape(LANES, LANES) for q in range(3)], axis=0)
                for c in range(2)
            ],
            axis=1,
        )
        real = imag = None
        for k in range(VBINS):
            prod = jnp.dot(band_t[t, k], rhs, preferred_element_type=F32)
            weight = tab_c[t, k]
            re = weight * (prod[:LANES, :LANES] - prod[LANES:, LANES:])
            im = weight * (prod[:LANES, LANES:] + prod[LANES:, :LANES])
            real = re if k == 0 else real + re
            imag = im if k == 0 else imag + im
        return real.astype(BF16), imag.astype(BF16)

    rows_n = spread(taps, None, True)
    build_n(0, rows_n)
    loads[2].wait()
    loads[3].wait()
    table_rows(0)
    loads[1].wait()
    first = over_r(lambda c, n: wave_v[c, :, pl.ds(LANES * n, LANES)], 0, 2)
    for c in range(2):
        for n in range(nt):
            send1[n, c] = first[c][n].astype(BF16)
    ubuf[1, xc] = send1[xc]

    @pl.when(y == 0)
    def _():
        ubuf[0] = jnp.zeros_like(ubuf[0])
        vbuf[0] = jnp.zeros_like(vbuf[0])

    @pl.when(y == last)
    def _():
        ubuf[2] = jnp.zeros_like(ubuf[2])
        vbuf[2] = jnp.zeros_like(vbuf[2])

    pl.semaphore_wait(barrier, 3 * (nt - 1))

    out1 = []
    for k in range(1, nt):
        to = (xc + k) % nt
        copy = remote(send1.at[to], ubuf.at[1, xc], s1.at[k - 1], r1.at[xc], dev(y, to, z))
        copy.start()
        out1.append(copy)

    def halo(piece, d):
        return remote(
            ubuf.at[1, piece], ubuf.at[2 - 2 * d, piece], hs.at[d, piece], hr.at[d, piece],
            dev((y + last + 2 * d) % nt, xc, z),
        )

    def pass_on(piece):
        @pl.when(y > 0)
        def _():
            halo(piece, 0).start()

        @pl.when(y < last)
        def _():
            halo(piece, 1).start()

    pass_on(xc)
    rows_t = spread(taps, None, False)
    build_t(0, rows_t)
    table_cols(0)
    loads[4].wait()
    row_pick = jnp.where(
        iota((LANES, nt * LANES // BLK), 1) == iota((LANES, nt * LANES // BLK), 0) // BLK + (LANES // BLK) * y, 1.0, 0.0
    ).astype(BF16)
    col_pick = one_hot(
        nt * LANES // BLK, LANES, iota((nt * LANES // BLK, LANES), 1) // BLK + (LANES // BLK) * xc
    )
    picked = jnp.dot(row_pick, ap_v[0].astype(BF16), preferred_element_type=F32).astype(BF16)
    mask_s[...] = jnp.dot(picked, col_pick, preferred_element_type=F32)

    for k in range(1, nt):
        piece = (xc + k) % nt
        remote(send1.at[piece], ubuf.at[1, piece], s1.at[k - 1], r1.at[piece], dev(y, piece, z)).wait_recv()
        pass_on(piece)

    @pl.when(y == z)
    def _():
        for k in range(1, nt):
            pl.semaphore_signal(hub_sem, inc=1, device_id=dev(y, xc, (z + k) % nt), device_id_type=MESH)

    @pl.when(y > 0)
    def _():
        for piece in range(nt):
            halo(piece, 1).wait_recv()

    @pl.when(y < last)
    def _():
        for piece in range(nt):
            halo(piece, 0).wait_recv()

    second = over_s(ubuf, 0)
    keep = mask_s[...] > 0.5
    for c in range(2):
        vbuf[1, :, c] = jnp.where(keep, second[c], jnp.zeros_like(second[c])).reshape(nt, sb, LANES)

    def halo3(d):
        return remote(
            vbuf.at[1], vbuf.at[2 - 2 * d], gs.at[d], gr.at[d], dev((y + last + 2 * d) % nt, xc, z)
        )

    @pl.when(y > 0)
    def _():
        halo3(0).start()

    @pl.when(y < last)
    def _():
        halo3(1).start()

    build_t(1, rows_t)
    table_cols(1)
    real = jnp.where(keep, second[0], jnp.zeros_like(second[0])).astype(F32)
    ssend[...] = jnp.transpose(real).astype(BF16).reshape(nt, sb, LANES)

    @pl.when(y != z)
    def _():
        pl.semaphore_wait(hub_sem, 1)

    def shallow(rho):
        return remote(ssend.at[rho], srecv.at[z], s6.at[rho], r6.at[z], dev(xc, rho, y))

    def shallow_here(rho):
        return pltpu.make_async_copy(ssend.at[rho], srecv.at[z], r6.at[z])

    for rho in range(nt):
        mine = (z == y) & (xc == y) & (xc == rho)

        @pl.when(mine)
        def _():
            shallow_here(rho).start()

        @pl.when(jnp.logical_not(mine))
        def _():
            shallow(rho).start()

    @pl.when(y > 0)
    def _():
        halo3(1).wait_recv()

    @pl.when(y < last)
    def _():
        halo3(0).wait_recv()

    third = over_s(vbuf, 1)
    for c in range(2):
        send4[:, c] = third[c].reshape(nt, sb, LANES)
    out4 = []
    for k in range(1, nt):
        to = (xc + k) % nt
        copy = remote(send4.at[to], rbuf.at[xc], s4.at[k - 1], r4.at[xc], dev(y, to, z))
        copy.start()
        out4.append(copy)
    rbuf[xc] = send4[xc]
    build_n(1, rows_n)
    table_rows(1)
    blocks = nt * LANES // BLK
    row_pick = jnp.where(
        iota((sb, blocks), 1) == iota((sb, blocks), 0) // BLK + (sb // BLK) * w, 1.0, 0.0
    ).astype(BF16)
    picked = jnp.dot(row_pick, ap_v[1].astype(BF16), preferred_element_type=F32).astype(BF16)
    mask_d[...] = jnp.dot(
        picked, one_hot(blocks, nt * LANES, iota((blocks, nt * LANES), 1) // BLK), preferred_element_type=F32
    )
    for k in range(1, nt):
        piece = (xc + k) % nt
        remote(send4.at[piece], rbuf.at[piece], s4.at[k - 1], r4.at[piece], dev(y, piece, z)).wait_recv()

    fourth = over_r(lambda c, n: rbuf[n, c], 1, 1)[0]
    for n in range(nt):
        keep_n = mask_d[:, pl.ds(LANES * n, LANES)] > 0.5
        tile = fourth[n].astype(BF16)
        dsend[n] = jnp.where(keep_n, tile, jnp.zeros_like(tile))
    out5 = []
    for k in range(1, nt):
        to = (z + k) % nt
        copy = remote(dsend.at[to], drecv.at[z], s5.at[k - 1], r5.at[z], dev(y, xc, to))
        copy.start()
        out5.append(copy)
    drecv[z] = dsend[z]

    for copy in out1 + out4:
        copy.wait_send()

    @pl.when(y > 0)
    def _():
        for piece in range(nt):
            halo(piece, 0).wait_send()
        halo3(0).wait_send()

    @pl.when(y < last)
    def _():
        for piece in range(nt):
            halo(piece, 1).wait_send()
        halo3(1).wait_send()

    for rho in range(nt):
        mine = (z == y) & (xc == y) & (xc == rho)

        @pl.when(jnp.logical_not(mine))
        def _():
            shallow(rho).wait_send()

    for f in range(nt):
        pltpu.make_async_copy(ssend.at[0], srecv.at[f], r6.at[f]).wait()
    shal_o[...] = jnp.sum(srecv[...].astype(F32), axis=0)

    for k in range(1, nt):
        f = (z + k) % nt
        remote(dsend.at[f], drecv.at[f], s5.at[k - 1], r5.at[f], dev(y, xc, f)).wait_recv()
    deep_o[...] = jnp.sum(drecv[...].astype(F32), axis=0)
    for copy in out5:
        copy.wait_send()


def solution(mesh):
    nt = mesh.shape["freq"]
    assert mesh.shape["wide"] == nt * nt
    sb = LANES // nt
    pos = nt * LANES

    def body(wave, filters, vel_bins, blend_levels, aperture):
        wave = wave.reshape(2, sb, pos)
        filters = jnp.transpose(filters, (0, 2, 3, 1, 4)).reshape(2, VBINS, 2, TAPS * TAPS)
        vel_bins = jnp.swapaxes(vel_bins, 1, 2)
        blend_levels = jnp.swapaxes(blend_levels, 1, 2)
        dma = pltpu.SemaphoreType.DMA
        return pl.pallas_call(
            functools.partial(kernel, nt),
            out_shape=(jax.ShapeDtypeStruct((sb, LANES), F32),) * 2,
            in_specs=[pl.BlockSpec(memory_space=pl.ANY)] * 5,
            out_specs=(pl.BlockSpec(memory_space=pltpu.VMEM),) * 2,
            scratch_shapes=[
                pltpu.VMEM(wave.shape, BF16),
                pltpu.VMEM(filters.shape, BF16),
                pltpu.VMEM(vel_bins.shape, jnp.int32),
                pltpu.VMEM(blend_levels.shape, jnp.int32),
                pltpu.VMEM(aperture.shape, jnp.int32),
                pltpu.VMEM((16, LANES), F32),
                pltpu.VMEM((2, VBINS, WIN, 2 * LANES), BF16),
                pltpu.VMEM((2, VBINS, 2 * LANES, WIN), BF16),
                pltpu.VMEM((2, 8, pos), F32),
                pltpu.VMEM((2, VBINS, LANES, LANES), F32),
                pltpu.VMEM((LANES, LANES), F32),
                pltpu.VMEM((sb, pos), F32),
                pltpu.VMEM((nt, 2, sb, LANES), BF16),
                pltpu.VMEM((3, nt, 2, sb, LANES), BF16),
                pltpu.VMEM((3, nt, 2, sb, LANES), BF16),
                pltpu.VMEM((nt, 2, sb, LANES), BF16),
                pltpu.VMEM((nt, 2, sb, LANES), BF16),
                pltpu.VMEM((nt, sb, LANES), BF16),
                pltpu.VMEM((nt, sb, LANES), BF16),
                pltpu.VMEM((nt, sb, LANES), BF16),
                pltpu.VMEM((nt, sb, LANES), BF16),
                dma((5,)),
                dma((nt,)),
                dma((nt,)),
                dma((2, nt)),
                dma((2, nt)),
                dma((2,)),
                dma((2,)),
                dma((nt,)),
                dma((nt,)),
                dma((nt,)),
                dma((nt,)),
                dma((nt,)),
                dma((nt,)),
                pltpu.SemaphoreType.REGULAR,
            ],
            compiler_params=pltpu.CompilerParams(collective_id=0, has_side_effects=True),
            name="sink",
        )(wave, filters, vel_bins, blend_levels, aperture)

    return jax.shard_map(
        body,
        mesh=mesh,
        in_specs=(P(None, "freq", "wide", None), P(None, None, "freq", None, None), P(), P(), P()),
        out_specs=(P("wide", "freq"), P("wide", "freq")),
        check_vma=False,
    )
```

time: 119 us -> 37.7 us (0.32); the launches traced: 117 us -> 37.5 us
  local copies, waits for them, and re-layouts: 47 us -> 1.9 us
  starting transfers between devices: 35.8 us -> 0 us
  Pallas kernels: 0 us -> 35 us
  waiting for transfers between devices: 18.7 us -> 0 us
  other arithmetic: 8.41 us -> 0 us
  matrix products: 6.25 us -> 0 us
    all_to_all x4 -> x0, starting transfers between devices: 35.8 us -> none  [the longest x2 13.7 us: summed_on_arrival(): lax.all_to_all(blocks, axis, split_axis=0, concat_axis=0, tiled=True)]
    pallas_call x0 -> x1, Pallas kernels: none -> 35 us  [body(): pl.pallas_call(functools.partial(kernel, nt), out_shape=(jax.ShapeDtypeSt...]
    another operation x23 -> x0, local copies, waits for them, and re-layouts: 21.3 us -> none
    all_to_all x4 -> x0, waiting for transfers between devices: 18.7 us -> none  [the longest x1 9.45 us: body(): lax.all_to_all(third, 'wide', split_axis=3, concat_axis=2, tiled=True)]
    unnamed x52 -> x4, local copies, waits for them, and re-layouts: 8.76 us -> 1.9 us
    dot_general x8 -> x0, matrix products: 6.25 us -> none  [the longest x4 4.09 us: spread(): banded = jnp.einsum('iya,jxb,kab->kijyx', row_pick, col_pick, taps_grid)]
    reshape x4 -> x0, local copies, waits for them, and re-layouts: 4.82 us -> none  [banded_bins(): jnp.transpose(pieces, (1, 2, 0, 3, 4))]
    convert_element_type x8 -> x0, local copies, waits for them, and re-layouts: 3.84 us -> none  [the longest x4 3.61 us: banded_bins(): matrix = jnp.transpose(matrix, (0, 3, 1, 2, 4)).reshape(2 * window * SIDE...]
  transfers between devices with their start and end apart: 4 -> 0, of which waited for: 3 -> 0; matrix products, arithmetic and copies ran while one was open for 26% -> 0% of each run, Pallas kernels for 0% -> 0%
where the time goes in v1:
time: 37.7 us; the launch traced here: 37.5 us
  Pallas kernels  35 us (93%)
  local copies, waits for them, and re-layouts  1.9 us (5%)
  between operations  0.65 us (2%)
    pallas_call x1, Pallas kernels, body(): pl.pallas_call(functools.partial(kernel, nt), out_shape=(jax.ShapeDtypeSt...  35 us
    unnamed x4, local copies, waits for them, and re-layouts  1.9 us

profile of v1, /device:TPU:1, one launch (start us, length us, event | category | flops | bytes accessed | tf_op | source)
XLA Modules:
  0.0 37.5 jit_solution(16014216972676329545)
XLA Ops:
  0.6 35.0 %sink.1 = (f32[16,128]{1,0:T(8,128)}, f32[16,128]{1,0:T(8,128)}) custom-call(bf16[2,16,1024]{2,1,0:T(8,128)(2,1)} %bitcast.8, bf16[2,3,2,81]{3,2,1,0:T(2,128)(2,1)} %bitcast.11, s32[2,3,2,1024]{3,2,1,0:T(2,128)} %bitcast.9, s32[2,3,2,1024]{3,2,1,0:T(2,128)} %bitcast.10, s32[2,64,64]{2,1,0:T(8,128)} %ap_h.1), custom_call_target="tpu_custom_call" | custom-call | tf_op jit(solution)/shard_map/sink/pallas_call | solution.py:385
  35.6 0.0 copy-start
  35.6 1.3 %copy.10 = f32[16,128]{1,0:T(8,128)} copy(f32[16,128]{1,0:T(8,128)} %get-tuple-element.4) | data formatting | bytes 16384
  36.9 0.0 copy-done
  36.9 0.6 %copy.11 = f32[16,128]{1,0:T(8,128)} copy(f32[16,128]{1,0:T(8,128)S(1)} %copy-done) | data formatting | bytes 16384
Async XLA Ops:
  35.6 1.3 %copy-start = (f32[16,128]{1,0:T(8,128)S(1)}, f32[16,128]{1,0:T(8,128)}, u32[]{:S(2)}) copy-start(f32[16,128]{1,0:T(8,128)} %get-tuple-element.5) | copy-start | bytes 24580

commit v2 on v1

v2 whole, which is shorter than its diff:
```python
import functools

import jax
import jax.numpy as jnp
from jax import lax
from jax.experimental import pallas as pl
from jax.experimental.pallas import tpu as pltpu
from jax.sharding import PartitionSpec as P

SIDE = 32
TAPS = 9
VBINS = 3
BLK = 16
LANES = 128
WIN = 3 * LANES
HALF = TAPS // 2
MESH = pl.DeviceIdType.MESH
F32 = jnp.float32
BF16 = jnp.bfloat16


def iota(shape, dim):
    return lax.broadcasted_iota(jnp.int32, shape, dim)


def one_hot(rows, cols, target):
    return jnp.where(iota((rows, cols), 0) == target, 1.0, 0.0).astype(BF16)


def kernel(
    nt, wave_h, filt_h, bins_h, lev_h, ap_h, shal_o, deep_o,
    wave_v, filt_v, bins_v, lev_v, ap_v, taps_v, band_n, blend_2, blend_3, tab_r, mask_s, mask_d,
    send1, ubuf, send2, rbuf, dsend, drecv, ssend, srecv,
    in_sem, s1, r1, s2, r2, s5, r5, s6, r6, met1, met2, met3,
):
    sb = LANES // nt
    nx = nt // 2
    w = lax.axis_index("wide")
    z = lax.axis_index("freq")
    y = w // nt
    xc = w % nt
    last = nt - 1

    def dev(yy, cc, zz):
        return (yy * nt + cc, zz)

    def remote(src, dst, ssem, rsem, to):
        return pltpu.make_async_remote_copy(
            src_ref=src, dst_ref=dst, send_sem=ssem, recv_sem=rsem, device_id=to, device_id_type=MESH
        )

    def signal(sem, to):
        pl.semaphore_signal(sem, inc=1, device_id=to, device_id_type=MESH)

    steps = sorted(((i, j) for i in range(nx) for j in range(2)), key=lambda s: (-min(s[0], nx - s[0]), -s[1]))

    def column(i, j):
        return (xc // 2 + i) % nx * 2 + (xc % 2 + j) % 2

    others = [column(i, j) for i, j in steps if (i, j) != (0, 0)]
    beside = sorted({1, last})
    two_off = sorted({2 % nt, (nt - 2) % nt} - {0})

    barrier = pltpu.get_barrier_semaphore()
    for k in beside:
        signal(barrier, dev(y, xc, (z + k) % nt))
        for c in others + [xc]:
            signal(barrier, dev((y + k) % nt, c, z))
    for c in others:
        signal(barrier, dev(y, c, z))

    loads = [
        pltpu.make_async_copy(h, v, in_sem.at[i])
        for i, (h, v) in enumerate(
            ((filt_h, filt_v), (wave_h, wave_v), (bins_h, bins_v), (lev_h, lev_v), (ap_h, ap_v))
        )
    ]
    for load in loads:
        load.start()

    taps_v[...] = jnp.zeros_like(taps_v)
    near = jnp.abs(iota((SIDE, LANES), 1) % SIDE - iota((SIDE, LANES), 0)) <= HALF

    def pick(flip):
        cols = iota((1, 12 * LANES), 1)
        group, m = cols // LANES, (cols + HALF) % LANES
        step, off = m // SIDE, m % SIDE
        a, b = (group - step, 2 * HALF - off) if flip else (4 * (group % 3) + step - group // 3, off)
        good = (a >= 0) & (a < TAPS) & (b >= 0) & (b < TAPS)
        return one_hot(LANES, 12 * LANES, jnp.where(good, a * TAPS + b, -1))

    pick_n = pick(True)
    loads[0].wait()
    for t in range(2):
        for k in range(VBINS):
            taps_v[pl.ds(2 * (VBINS * t + k), 2), pl.ds(0, TAPS * TAPS)] = filt_v[t, k].astype(F32)
    taps = taps_v[...].astype(BF16)

    def banded(rows, r, g):
        wide = jnp.broadcast_to(rows[r : r + 1, LANES * g : LANES * (g + 1)], (SIDE, LANES))
        return pltpu.roll(wide, 0, 1, stride=1, stride_axis=0)

    def build_n(t, rows):
        for part in range(2):
            for k in range(VBINS):
                r = 2 * (VBINS * t + k) + part
                for i in range(12):
                    band_n[t, k, pl.ds(SIDE * i, SIDE), pl.ds(LANES * part, LANES)] = jnp.where(
                        near, banded(rows, r, i), 0.0
                    ).astype(BF16)

    def blended(t, rows, part, j, q, cols):
        total = None
        for k in range(VBINS):
            term = cols[k][SIDE * j : SIDE * (j + 1)] * banded(rows, 2 * (VBINS * t + k) + part, 3 * j + q)
            total = term if k == 0 else total + term
        return jnp.where(near, total, 0.0).astype(BF16)

    def table(t, q, cols):
        bin_ids = [bins_v[t, j, pl.ds(q, 1), cols] for j in range(VBINS)]
        levels = [lev_v[t, j, pl.ds(q, 1), cols].astype(F32) for j in range(VBINS)]
        total = levels[0] + levels[1] + levels[2]
        rows = []
        for k in range(VBINS):
            hits = [jnp.where(b == k, v, 0.0) for b, v in zip(bin_ids, levels)]
            rows.append((hits[0] + hits[1] + hits[2]) / total)
        return rows

    def table_rows(t):
        for k, row in enumerate(table(t, 0, slice(None))):
            tab_r[t, pl.ds(k, 1), :] = row

    def table_cols(t, tile):
        here = pl.ds(pl.multiple_of(tile * LANES, LANES), LANES)
        return [jnp.transpose(jnp.broadcast_to(row, (LANES, LANES))) for row in table(t, 1, here)]

    def over_r(field, t, parts):
        zero = jnp.zeros((sb, LANES), BF16)
        tiles = [[field(c, n) for n in range(nt)] for c in range(2)]
        rows = []
        for c in range(2):
            for n in range(nt):
                rows.append(
                    jnp.concatenate(
                        [tiles[c][m] if 0 <= m < nt else zero for m in (n - 1, n, n + 1)], axis=1
                    )
                )
        lhs = jnp.concatenate(rows, axis=0)
        out = [[None] * nt for _ in range(parts)]
        for k in range(VBINS):
            prod = jnp.dot(lhs, band_n[t, k], preferred_element_type=F32)
            for n in range(nt):
                weight = tab_r[t, pl.ds(k, 1), pl.ds(LANES * n, LANES)]
                top = slice(sb * n, sb * (n + 1))
                low = slice(sb * (nt + n), sb * (nt + n + 1))
                terms = [prod[top, :LANES] - prod[low, LANES:]]
                if parts == 2:
                    terms.append(prod[top, LANES:] + prod[low, :LANES])
                for c, term in enumerate(terms):
                    term = weight * term
                    out[c][n] = term if k == 0 else out[c][n] + term
        return out

    def complex_of(prod):
        return (
            (prod[:LANES, :LANES] - prod[LANES:, LANES:]).astype(BF16),
            (prod[:LANES, LANES:] + prod[LANES:, :LANES]).astype(BF16),
        )

    rows_n = jnp.dot(taps, pick_n, preferred_element_type=F32)
    build_n(0, rows_n)
    loads[2].wait()
    loads[3].wait()
    table_rows(0)
    loads[1].wait()
    first = over_r(lambda c, n: wave_v[c, :, pl.ds(LANES * n, LANES)], 0, 2)
    for c in range(2):
        for n in range(nt):
            send1[n, c] = first[c][n].astype(BF16)

    @pl.when(y == 0)
    def _():
        ubuf[0] = jnp.zeros_like(ubuf[0])
        rbuf[0] = jnp.zeros_like(rbuf[0])

    @pl.when(y == last)
    def _():
        ubuf[2] = jnp.zeros_like(ubuf[2])
        rbuf[2] = jnp.zeros_like(rbuf[2])

    pl.semaphore_wait(barrier, len(beside) * (nt + 1) + last)

    def to_row(d, start, copy):
        def run():
            for c in others + ([xc] if d else []):
                if start:
                    copy(1 - d, c).start()
                else:
                    copy(1 - d, c).wait_send()

        if d == 0:
            run()
        else:
            pl.when(y < last if d > 0 else y > 0)(run)

    def arrive(copy):
        def run(q):
            for c in others[::-1] + ([xc] if q != 1 else []):
                copy(q, c).wait_recv()

        run(1)
        pl.when(y > 0)(lambda: run(0))
        pl.when(y < last)(lambda: run(2))

    def there(q, c):
        return dev((y + 1 - q + nt) % nt, c, z)

    def copy1(q, c):
        return remote(send1.at[c], ubuf.at[q, xc], s1.at[q, c], r1.at[q, xc], there(q, c))

    def copy1_in(q, c):
        return remote(send1.at[c], ubuf.at[q, c], s1.at[q, c], r1.at[q, c], there(q, c))

    def copy2(q, c):
        return remote(send2.at[q, c], rbuf.at[q, xc], s2.at[q, c], r2.at[q, xc], there(q, c))

    def copy2_in(q, c):
        return remote(send2.at[q, c], rbuf.at[q, c], s2.at[q, c], r2.at[q, c], there(q, c))

    for d in (1, -1, 0):
        to_row(d, True, copy1)
    for k in beside:
        signal(met1, dev((y + k) % nt, xc, z))
        signal(met1, dev(y, xc, (z + k) % nt))
    ubuf[1, xc] = send1[xc]

    rows_t = jnp.dot(taps, pick(False), preferred_element_type=F32)
    cols = table_cols(0, y)
    for part in range(2):
        for j in range(4):
            for q in range(3):
                blend_2[pl.ds(LANES * part + SIDE * j, SIDE), pl.ds(LANES * q, LANES)] = blended(
                    0, rows_t, part, j, q, cols
                )
    blocks = nt * LANES // BLK
    per_tile = LANES // BLK
    loads[4].wait()
    row_pick = jnp.where(
        iota((LANES, blocks), 1) == iota((LANES, blocks), 0) // BLK + per_tile * y, 1.0, 0.0
    ).astype(BF16)
    col_pick = one_hot(blocks, LANES, iota((blocks, LANES), 1) // BLK + per_tile * xc)
    picked = jnp.dot(row_pick, ap_v[0].astype(BF16), preferred_element_type=F32).astype(BF16)
    mask_s[...] = jnp.dot(picked, col_pick, preferred_element_type=F32)

    pl.semaphore_wait(met1, 2 * len(beside))
    for k in two_off:
        signal(met2, dev((y + k) % nt, xc, z))
        signal(met2, dev(y, xc, (z + k) % nt))

    for q in range(3):
        cols = table_cols(1, (y + 1 - q + nt) % nt)
        for part in range(2):
            for j in range(4):
                blend_3[q, pl.ds(LANES * part + SIDE * j, SIDE), :] = blended(1, rows_t, part, j, q, cols)

    if two_off:
        pl.semaphore_wait(met2, 2 * len(two_off))
    for k in range(1, nt):
        signal(met3, dev(y, xc, (z + k) % nt))

    build_n(1, rows_n)
    table_rows(1)
    row_pick = jnp.where(
        iota((sb, blocks), 1) == iota((sb, blocks), 0) // BLK + (sb // BLK) * w, 1.0, 0.0
    ).astype(BF16)
    picked = jnp.dot(row_pick, ap_v[1].astype(BF16), preferred_element_type=F32).astype(BF16)
    mask_d[...] = jnp.dot(
        picked, one_hot(blocks, nt * LANES, iota((blocks, nt * LANES), 1) // BLK), preferred_element_type=F32
    )

    arrive(copy1_in)

    rhs = jnp.concatenate(
        [
            jnp.concatenate([ubuf[q, :, c].reshape(LANES, LANES) for q in range(3)], axis=0)
            for c in range(2)
        ],
        axis=1,
    )
    keep = mask_s[...] > 0.5
    field = [
        jnp.where(keep, part, jnp.zeros_like(part))
        for part in complex_of(jnp.dot(blend_2[...], rhs, preferred_element_type=F32))
    ]

    rhs = jnp.concatenate(field, axis=1)
    for d in (1, -1, 0):
        q = 1 - d
        for c, part in enumerate(complex_of(jnp.dot(blend_3[q], rhs, preferred_element_type=F32))):
            send2[q, :, c] = part.reshape(nt, sb, LANES)
        to_row(d, True, copy2)
    rbuf[1, xc] = send2[1, xc]

    ssend[...] = jnp.transpose(field[0].astype(F32)).astype(BF16).reshape(nt, sb, LANES)
    pl.semaphore_wait(met3, last)

    def shallow(rho):
        return remote(ssend.at[rho], srecv.at[z], s6.at[rho], r6.at[z], dev(xc, rho, y))

    def shallow_here(rho):
        return pltpu.make_async_copy(ssend.at[rho], srecv.at[z], r6.at[z])

    for rho in range(nt):
        mine = (z == y) & (xc == y) & (xc == rho)

        @pl.when(mine)
        def _():
            shallow_here(rho).start()

        @pl.when(jnp.logical_not(mine))
        def _():
            shallow(rho).start()

    arrive(copy2_in)

    def third(c, n):
        return (rbuf[0, n, c].astype(F32) + rbuf[1, n, c].astype(F32) + rbuf[2, n, c].astype(F32)).astype(BF16)

    fourth = over_r(third, 1, 1)[0]
    for n in range(nt):
        keep_n = mask_d[:, pl.ds(LANES * n, LANES)] > 0.5
        tile = fourth[n].astype(BF16)
        dsend[n] = jnp.where(keep_n, tile, jnp.zeros_like(tile))
    out5 = []
    for k in sorted(range(1, nt), key=lambda k: -min(k, nt - k)):
        to = (z + k) % nt
        copy = remote(dsend.at[to], drecv.at[z], s5.at[k - 1], r5.at[z], dev(y, xc, to))
        copy.start()
        out5.append(copy)
    drecv[z] = dsend[z]

    for d in (1, -1, 0):
        to_row(d, False, copy1)
        to_row(d, False, copy2)
    for rho in range(nt):
        mine = (z == y) & (xc == y) & (xc == rho)

        @pl.when(jnp.logical_not(mine))
        def _():
            shallow(rho).wait_send()

    for f in range(nt):
        pltpu.make_async_copy(ssend.at[0], srecv.at[f], r6.at[f]).wait()
    shal_o[...] = jnp.sum(srecv[...].astype(F32), axis=0)

    for k in range(1, nt):
        f = (z + k) % nt
        remote(dsend.at[f], drecv.at[f], s5.at[k - 1], r5.at[f], dev(y, xc, f)).wait_recv()
    deep_o[...] = jnp.sum(drecv[...].astype(F32), axis=0)
    for copy in out5:
        copy.wait_send()


def solution(mesh):
    nt = mesh.shape["freq"]
    assert mesh.shape["wide"] == nt * nt
    sb = LANES // nt
    pos = nt * LANES

    def body(wave, filters, vel_bins, blend_levels, aperture):
        wave = wave.reshape(2, sb, pos)
        filters = jnp.transpose(filters, (0, 2, 3, 1, 4)).reshape(2, VBINS, 2, TAPS * TAPS)
        vel_bins = jnp.swapaxes(vel_bins, 1, 2)
        blend_levels = jnp.swapaxes(blend_levels, 1, 2)
        dma = pltpu.SemaphoreType.DMA
        return pl.pallas_call(
            functools.partial(kernel, nt),
            out_shape=(jax.ShapeDtypeStruct((sb, LANES), F32),) * 2,
            in_specs=[pl.BlockSpec(memory_space=pl.ANY)] * 5,
            out_specs=(pl.BlockSpec(memory_space=pltpu.VMEM),) * 2,
            scratch_shapes=[
                pltpu.VMEM(wave.shape, BF16),
                pltpu.VMEM(filters.shape, BF16),
                pltpu.VMEM(vel_bins.shape, jnp.int32),
                pltpu.VMEM(blend_levels.shape, jnp.int32),
                pltpu.VMEM(aperture.shape, jnp.int32),
                pltpu.VMEM((16, LANES), F32),
                pltpu.VMEM((2, VBINS, WIN, 2 * LANES), BF16),
                pltpu.VMEM((2 * LANES, WIN), BF16),
                pltpu.VMEM((3, 2 * LANES, LANES), BF16),
                pltpu.VMEM((2, 8, pos), F32),
                pltpu.VMEM((LANES, LANES), F32),
                pltpu.VMEM((sb, pos), F32),
                pltpu.VMEM((nt, 2, sb, LANES), BF16),
                pltpu.VMEM((3, nt, 2, sb, LANES), BF16),
                pltpu.VMEM((3, nt, 2, sb, LANES), BF16),
                pltpu.VMEM((3, nt, 2, sb, LANES), BF16),
                pltpu.VMEM((nt, sb, LANES), BF16),
                pltpu.VMEM((nt, sb, LANES), BF16),
                pltpu.VMEM((nt, sb, LANES), BF16),
                pltpu.VMEM((nt, sb, LANES), BF16),
                dma((5,)),
                dma((3, nt)),
                dma((3, nt)),
                dma((3, nt)),
                dma((3, nt)),
                dma((nt,)),
                dma((nt,)),
                dma((nt,)),
                dma((nt,)),
                pltpu.SemaphoreType.REGULAR,
                pltpu.SemaphoreType.REGULAR,
                pltpu.SemaphoreType.REGULAR,
            ],
            compiler_params=pltpu.CompilerParams(collective_id=0, has_side_effects=True),
            name="sink",
        )(wave, filters, vel_bins, blend_levels, aperture)

    return jax.shard_map(
        body,
        mesh=mesh,
        in_specs=(P(None, "freq", "wide", None), P(None, None, "freq", None, None), P(), P(), P()),
        out_specs=(P("wide", "freq"), P("wide", "freq")),
        check_vma=False,
    )
```

time: 37.7 us -> 33 us (0.88)
  Pallas kernels: 35 us -> 30.3 us
    pallas_call x1, Pallas kernels: 35 us -> 30.3 us  [body(): pl.pallas_call(functools.partial(kernel, nt), out_shape=(jax.ShapeDtypeSt...]
where the time goes in v2:
time: 33 us; the launch traced here: 32.8 us
  Pallas kernels  30.3 us (92%)
  local copies, waits for them, and re-layouts  1.9 us (6%)
  between operations  0.65 us (2%)
    pallas_call x1, Pallas kernels, body(): pl.pallas_call(functools.partial(kernel, nt), out_shape=(jax.ShapeDtypeSt...  30.3 us
    unnamed x4, local copies, waits for them, and re-layouts  1.9 us

profile of v2, /device:TPU:1, one launch (start us, length us, event | category | flops | bytes accessed | tf_op | source)
XLA Modules:
  0.0 32.8 jit_solution(8696311791506005045)
XLA Ops:
  0.6 30.3 %sink.1 = (f32[16,128]{1,0:T(8,128)}, f32[16,128]{1,0:T(8,128)}) custom-call(bf16[2,16,1024]{2,1,0:T(8,128)(2,1)} %bitcast.8, bf16[2,3,2,81]{3,2,1,0:T(2,128)(2,1)} %bitcast.11, s32[2,3,2,1024]{3,2,1,0:T(2,128)} %bitcast.9, s32[2,3,2,1024]{3,2,1,0:T(2,128)} %bitcast.10, s32[2,64,64]{2,1,0:T(8,128)} %ap_h.1), custom_call_target="tpu_custom_call" | custom-call | tf_op jit(solution)/shard_map/sink/pallas_call | solution.py:376
  30.9 0.0 copy-start
  30.9 1.3 %copy.10 = f32[16,128]{1,0:T(8,128)} copy(f32[16,128]{1,0:T(8,128)} %get-tuple-element.4) | data formatting | bytes 16384
  32.2 0.0 copy-done
  32.2 0.6 %copy.11 = f32[16,128]{1,0:T(8,128)} copy(f32[16,128]{1,0:T(8,128)S(1)} %copy-done) | data formatting | bytes 16384
Async XLA Ops:
  30.9 1.3 %copy-start = (f32[16,128]{1,0:T(8,128)S(1)}, f32[16,128]{1,0:T(8,128)}, u32[]{:S(2)}) copy-start(f32[16,128]{1,0:T(8,128)} %get-tuple-element.5) | copy-start | bytes 24580

commit v3 on v2

--- a/solution.py
+++ b/solution.py
@@ -28,8 +28,8 @@
 
 
 def kernel(
-    nt, wave_h, filt_h, bins_h, lev_h, ap_h, shal_o, deep_o,
-    wave_v, filt_v, bins_v, lev_v, ap_v, taps_v, band_n, blend_2, blend_3, tab_r, mask_s, mask_d,
+    nt, wave_h, filt_h, bins_h, lev_h, ap_h, image_o,
+    wave_v, filt_v, bins_v, lev_v, ap_v, taps_v, band_1, band_4, blend_2, blend_3, tab_r, mask_s, mask_d,
     send1, ubuf, send2, rbuf, dsend, drecv, ssend, srecv,
     in_sem, s1, r1, s2, r2, s5, r5, s6, r6, met1, met2, met3,
 ):
@@ -61,14 +61,6 @@
     beside = sorted({1, last})
     two_off = sorted({2 % nt, (nt - 2) % nt} - {0})
 
-    barrier = pltpu.get_barrier_semaphore()
-    for k in beside:
-        signal(barrier, dev(y, xc, (z + k) % nt))
-        for c in others + [xc]:
-            signal(barrier, dev((y + k) % nt, c, z))
-    for c in others:
-        signal(barrier, dev(y, c, z))
-
     loads = [
         pltpu.make_async_copy(h, v, in_sem.at[i])
         for i, (h, v) in enumerate(
@@ -78,6 +70,14 @@
     for load in loads:
         load.start()
 
+    barrier = pltpu.get_barrier_semaphore()
+    for k in beside:
+        signal(barrier, dev(y, xc, (z + k) % nt))
+        for c in others + [xc]:
+            signal(barrier, dev((y + k) % nt, c, z))
+    for c in others:
+        signal(barrier, dev(y, c, z))
+
     taps_v[...] = jnp.zeros_like(taps_v)
     near = jnp.abs(iota((SIDE, LANES), 1) % SIDE - iota((SIDE, LANES), 0)) <= HALF
 
@@ -100,14 +100,12 @@
         wide = jnp.broadcast_to(rows[r : r + 1, LANES * g : LANES * (g + 1)], (SIDE, LANES))
         return pltpu.roll(wide, 0, 1, stride=1, stride_axis=0)
 
-    def build_n(t, rows):
+    def blocks_n(t, rows):
         for part in range(2):
             for k in range(VBINS):
                 r = 2 * (VBINS * t + k) + part
                 for i in range(12):
-                    band_n[t, k, pl.ds(SIDE * i, SIDE), pl.ds(LANES * part, LANES)] = jnp.where(
-                        near, banded(rows, r, i), 0.0
-                    ).astype(BF16)
+                    yield part, k, i, jnp.where(near, banded(rows, r, i), 0.0)
 
     def blended(t, rows, part, j, q, cols):
         total = None
@@ -134,32 +132,13 @@
         here = pl.ds(pl.multiple_of(tile * LANES, LANES), LANES)
         return [jnp.transpose(jnp.broadcast_to(row, (LANES, LANES))) for row in table(t, 1, here)]
 
-    def over_r(field, t, parts):
+    def windows(field):
         zero = jnp.zeros((sb, LANES), BF16)
-        tiles = [[field(c, n) for n in range(nt)] for c in range(2)]
-        rows = []
-        for c in range(2):
-            for n in range(nt):
-                rows.append(
-                    jnp.concatenate(
-                        [tiles[c][m] if 0 <= m < nt else zero for m in (n - 1, n, n + 1)], axis=1
-                    )
-                )
-        lhs = jnp.concatenate(rows, axis=0)
-        out = [[None] * nt for _ in range(parts)]
-        for k in range(VBINS):
-            prod = jnp.dot(lhs, band_n[t, k], preferred_element_type=F32)
-            for n in range(nt):
-                weight = tab_r[t, pl.ds(k, 1), pl.ds(LANES * n, LANES)]
-                top = slice(sb * n, sb * (n + 1))
-                low = slice(sb * (nt + n), sb * (nt + n + 1))
-                terms = [prod[top, :LANES] - prod[low, LANES:]]
-                if parts == 2:
-                    terms.append(prod[top, LANES:] + prod[low, :LANES])
-                for c, term in enumerate(terms):
-                    term = weight * term
-                    out[c][n] = term if k == 0 else out[c][n] + term
-        return out
+        tiles = [zero] + [field(n) for n in range(nt)] + [zero]
+        return jnp.concatenate([jnp.concatenate(tiles[n : n + 3], axis=1) for n in range(nt)], axis=0)
+
+    def weight(t, k, n):
+        return tab_r[t, pl.ds(k, 1), pl.ds(LANES * n, LANES)]
 
     def complex_of(prod):
         return (
@@ -168,12 +147,25 @@
         )
 
     rows_n = jnp.dot(taps, pick_n, preferred_element_type=F32)
-    build_n(0, rows_n)
+    for part, k, i, block in blocks_n(0, rows_n):
+        band_1[k, pl.ds(SIDE * i, SIDE), pl.ds(LANES * part, LANES)] = block.astype(BF16)
     loads[2].wait()
     loads[3].wait()
     table_rows(0)
     loads[1].wait()
-    first = over_r(lambda c, n: wave_v[c, :, pl.ds(LANES * n, LANES)], 0, 2)
+    lhs = jnp.concatenate(
+        [windows(lambda n: wave_v[c, :, pl.ds(LANES * n, LANES)]) for c in range(2)], axis=0
+    )
+    first = [[None] * nt for _ in range(2)]
+    for k in range(VBINS):
+        prod = jnp.dot(lhs, band_1[k], preferred_element_type=F32)
+        for n in range(nt):
+            top = prod[sb * n : sb * (n + 1)]
+            low = prod[sb * (nt + n) : sb * (nt + n + 1)]
+            terms = (top[:, :LANES] - low[:, LANES:], top[:, LANES:] + low[:, :LANES])
+            for c, term in enumerate(terms):
+                term = weight(0, k, n) * term
+                first[c][n] = term if k == 0 else first[c][n] + term
     for c in range(2):
         for n in range(nt):
             send1[n, c] = first[c][n].astype(BF16)
@@ -268,7 +260,9 @@
     for k in range(1, nt):
         signal(met3, dev(y, xc, (z + k) % nt))
 
-    build_n(1, rows_n)
+    for part, k, i, block in blocks_n(1, rows_n):
+        rows = pl.ds(WIN * part + SIDE * i, SIDE)
+        band_4[rows, pl.ds(LANES * k, LANES)] = (block if part == 0 else -block).astype(BF16)
     table_rows(1)
     row_pick = jnp.where(
         iota((sb, blocks), 1) == iota((sb, blocks), 0) // BLK + (sb // BLK) * w, 1.0, 0.0
@@ -326,17 +320,22 @@
     def third(c, n):
         return (rbuf[0, n, c].astype(F32) + rbuf[1, n, c].astype(F32) + rbuf[2, n, c].astype(F32)).astype(BF16)
 
-    fourth = over_r(third, 1, 1)[0]
+    lhs = jnp.concatenate([windows(functools.partial(third, c)) for c in range(2)], axis=1)
+    prod = jnp.dot(lhs, band_4[...], preferred_element_type=F32)
     for n in range(nt):
+        rows = prod[sb * n : sb * (n + 1)]
+        tile = weight(1, 0, n) * rows[:, :LANES]
+        for k in range(1, VBINS):
+            tile = tile + weight(1, k, n) * rows[:, LANES * k : LANES * (k + 1)]
+        tile = tile.astype(BF16)
         keep_n = mask_d[:, pl.ds(LANES * n, LANES)] > 0.5
-        tile = fourth[n].astype(BF16)
         dsend[n] = jnp.where(keep_n, tile, jnp.zeros_like(tile))
-    out5 = []
-    for k in sorted(range(1, nt), key=lambda k: -min(k, nt - k)):
-        to = (z + k) % nt
-        copy = remote(dsend.at[to], drecv.at[z], s5.at[k - 1], r5.at[z], dev(y, xc, to))
-        copy.start()
-        out5.append(copy)
+
+    def deep(f):
+        return remote(dsend.at[f], drecv.at[z], s5.at[f], r5.at[z], dev(y, xc, f))
+
+    for f in range(nt):
+        pl.when(z != f)(deep(f).start)
     drecv[z] = dsend[z]
 
     for d in (1, -1, 0):
@@ -351,14 +350,13 @@
 
     for f in range(nt):
         pltpu.make_async_copy(ssend.at[0], srecv.at[f], r6.at[f]).wait()
-    shal_o[...] = jnp.sum(srecv[...].astype(F32), axis=0)
-
-    for k in range(1, nt):
-        f = (z + k) % nt
-        remote(dsend.at[f], drecv.at[f], s5.at[k - 1], r5.at[f], dev(y, xc, f)).wait_recv()
-    deep_o[...] = jnp.sum(drecv[...].astype(F32), axis=0)
-    for copy in out5:
-        copy.wait_send()
+    image_o[0] = jnp.sum(srecv[...].astype(F32), axis=0)
+
+    for f in range(nt):
+        pl.when(z != f)(remote(dsend.at[f], drecv.at[f], s5.at[f], r5.at[f], dev(y, xc, f)).wait_recv)
+    image_o[1] = jnp.sum(drecv[...].astype(F32), axis=0)
+    for f in range(nt):
+        pl.when(z != f)(deep(f).wait_send)
 
 
 def solution(mesh):
@@ -373,11 +371,11 @@
         vel_bins = jnp.swapaxes(vel_bins, 1, 2)
         blend_levels = jnp.swapaxes(blend_levels, 1, 2)
         dma = pltpu.SemaphoreType.DMA
-        return pl.pallas_call(
+        images = pl.pallas_call(
             functools.partial(kernel, nt),
-            out_shape=(jax.ShapeDtypeStruct((sb, LANES), F32),) * 2,
+            out_shape=pltpu.VMEM((2, sb, LANES), F32),
             in_specs=[pl.BlockSpec(memory_space=pl.ANY)] * 5,
-            out_specs=(pl.BlockSpec(memory_space=pltpu.VMEM),) * 2,
+            out_specs=pl.BlockSpec(memory_space=pltpu.VMEM),
             scratch_shapes=[
                 pltpu.VMEM(wave.shape, BF16),
                 pltpu.VMEM(filters.shape, BF16),
@@ -385,7 +383,8 @@
                 pltpu.VMEM(blend_levels.shape, jnp.int32),
                 pltpu.VMEM(aperture.shape, jnp.int32),
                 pltpu.VMEM((16, LANES), F32),
-                pltpu.VMEM((2, VBINS, WIN, 2 * LANES), BF16),
+                pltpu.VMEM((VBINS, WIN, 2 * LANES), BF16),
+                pltpu.VMEM((2 * WIN, VBINS * LANES), BF16),
                 pltpu.VMEM((2 * LANES, WIN), BF16),
                 pltpu.VMEM((3, 2 * LANES, LANES), BF16),
                 pltpu.VMEM((2, 8, pos), F32),
@@ -415,6 +414,7 @@
             compiler_params=pltpu.CompilerParams(collective_id=0, has_side_effects=True),
             name="sink",
         )(wave, filters, vel_bins, blend_levels, aperture)
+        return images[0], images[1]
 
     return jax.shard_map(
         body,

time: 33 us -> 30.6 us (0.927)
  the two profiles are of different devices: /device:TPU:1 before, /device:TPU:8 now
where the time goes in v3:
time: 30.6 us; the launch traced here: 30.4 us
  Pallas kernels  29.2 us (95%)
  between operations  0.64 us (2%)
  local copies, waits for them, and re-layouts  0.61 us (2%)
    pallas_call x1, Pallas kernels, body(): pl.pallas_call(functools.partial(kernel, nt), out_shape=pltpu.VMEM((2, sb...  29.2 us

profile of v3, /device:TPU:8, one launch (start us, length us, event | category | flops | bytes accessed | tf_op | source)
XLA Modules:
  0.0 30.4 jit_solution(7257611701195765849)
XLA Ops:
  0.6 29.2 %sink.1 = f32[2,16,128]{2,1,0:T(8,128)S(1)} custom-call(bf16[2,16,1024]{2,1,0:T(8,128)(2,1)} %bitcast.12, bf16[2,3,2,81]{3,2,1,0:T(2,128)(2,1)} %bitcast.15, s32[2,3,2,1024]{3,2,1,0:T(2,128)} %bitcast.13, s32[2,3,2,1024]{3,2,1,0:T(2,128)} %bitcast.14, s32[2,64,64]{2,1,0:T(8,128)} %ap_h.1), custom_call_target="tpu_custom_call" | custom-call | tf_op jit(solution)/shard_map/sink/pallas_call | solution.py:374
  29.8 0.6 %slice_bitcast_fusion = (f32[16,128]{1,0:T(8,128)}, f32[16,128]{1,0:T(8,128)}) fusion(f32[2,16,128]{2,1,0:T(8,128)S(1)} %sink.1), kind=kLoop, calls=%fused_computation | loop fusion | bytes 32768 | tf_op jit(solution)/shard_map/squeeze | solution.py:417
